TPU v7x, 32 devices: a whole 2x2x4 slice. The times are simulated.
32 devices in a mesh: px: 4 (over x, core), py: 8 (over z, y).
Axes of the slice: x: 2, y: 2, z: 4, core: 2. Of those that a mesh axis runs over, the one named last changes fastest.
Arguments:
- displacement: float32 [3, 131072], P(None, ('px', 'py')), may hold values from -6 to 6
- disp_prev: float32 [3, 131072], P(None, ('px', 'py')), may hold values from -6 to 6
- nodal_load: float32 [3, 131072], P(None, ('px', 'py')), may hold values from -6 to 6
- nodal_mass: float32 [131072], P(('px', 'py')), may hold values from 1 to 4
- modulus: float32 [16384], P(('px', 'py')), may hold values from 1 to 10
- stiffness: float32 [81, 81], replicated
- connectivity: int32 [27, 16384], P(None, ('px', 'py')), may hold values from 0 to 4607, as said below
- ghost_send: int32 [2, 8192], P(None, ('px', 'py')), may hold values from 0 to 4095
- contact_node: int32 [65536], P(('px', 'py')), may hold values from 0 to 4095
- contact_owner: int32 [65536], P(('px', 'py')), may hold values from 0 to 31, as said below
- pair_ids: int32 [2, 32768], P(None, ('px', 'py')), may hold values from 0 to 4095
- gap_start: float32 [3, 32768], P(None, ('px', 'py')), may hold values from -3 to 3
- penalty: float32 [32768], P(('px', 'py')), may hold values from 0.5 to 2
- friction: float32 [32768], P(('px', 'py')), may hold values from 0.2 to 0.6
- slip_state: int32 [3, 32768], P(None, ('px', 'py')), may hold values 0 or 1
Outputs:
- new_displacement: float32 [3, 131072], P(None, ('px', 'py'))
- acceleration: float32 [3, 131072], P(None, ('px', 'py'))
Inputs may be any that keep to these rules, and one draw needn't show every extreme that they name: `connectivity`: of each device's 512 elements, the first 384 name only the device's own nodes, indices below 4096; the others name own and ghost nodes. `contact_owner`: among the 2048 contact nodes of one device at most 128 name the same owner; one owner is named by exactly 128 nodes of every device.
All inputs are finite; a program needn't handle non-finite values. No bound on the sum of `slip_state` on one device may be relied on, other than what follows from the above.
Results may differ from a plain program's by a relative error of at most 0.0003.
Values sent between devices are 32-bit elements; how exact they have to be, the bound alone decides.
A program may use at most 64 MiB of HBM per device.

v0:
```python
import functools

import jax
import jax.numpy as jnp
from jax import lax
from jax.experimental import pallas as pl
from jax.experimental.pallas import tpu as pltpu
from jax.sharding import PartitionSpec as P

STEPS = 3
LANES = 128
SUBLANES = 8
MESH = pl.DeviceIdType.MESH

time_step_sq = 0.05


def matches(index_row, rows):
    return lax.broadcasted_iota(jnp.int32, (rows, index_row.shape[1]), 0) == index_row


def split(value):
    high = value.astype(jnp.bfloat16)
    return high, (value - high.astype(jnp.float32)).astype(jnp.bfloat16)


def side_by_side(table):
    return jnp.concatenate(split(table), axis=1)


def gather(table, lane_hot, row_index, rows):
    got = jnp.dot(
        table,
        jnp.concatenate([lane_hot, lane_hot], axis=0),
        preferred_element_type=jnp.float32,
    )
    mask = matches(row_index, rows)
    return [
        jnp.sum(jnp.where(mask, got[c * rows : (c + 1) * rows], 0.0), axis=0, keepdims=True)
        for c in range(3)
    ]


def scatter(values, lane_hot, row_index, rows):
    mask = matches(row_index, rows)
    parts = [split(value) for value in values]
    left = jnp.concatenate(
        [jnp.where(mask, parts[c][s].astype(jnp.float32), 0.0) for s in range(2) for c in range(3)],
        axis=0,
    ).astype(jnp.bfloat16)
    return lax.dot_general(
        left, lane_hot, (((1,), (1,)), ((), ())), preferred_element_type=jnp.float32
    )


def kernel(
    dims,
    idx,
    owner,
    node,
    mod,
    stiff,
    gap0,
    pen,
    fric,
    slip,
    disp,
    prev,
    load,
    mass,
    out_u,
    out_a,
    row_of,
    lane_hot,
    own_tab,
    ext,
    ext_tab,
    ue,
    fe,
    acc_e,
    acc_c,
    slot_vals,
    pair_vals,
    recv_tab,
    cur,
    old,
    box_out,
    box_in,
    halo_out,
    halo_in,
    box_send,
    box_recv,
    halo_send,
    halo_recv,
):
    n_py, n, cap, elnode, lent, width = dims
    px, py = lax.axis_index("px"), lax.axis_index("py")
    me = px * n_py + py

    def place(device):
        return {"px": lax.div(device, n_py), "py": lax.rem(device, n_py)}

    barrier = pltpu.get_barrier_semaphore()

    @pl.loop(1, n)
    def _(d):
        pl.semaphore_signal(
            barrier, inc=1, device_id=place(lax.rem(me + d, n)), device_id_type=MESH
        )

    own_rows = cur.shape[0] // 3
    ext_rows = ext.shape[0] // 3
    slots = slot_vals.shape[1]
    slot_rows = recv_tab.shape[0] // 3
    given = idx.shape[0]
    lend = elnode
    pair_chunks = pen.shape[1] // width
    near, far = elnode + 1, elnode + 1 + pair_chunks

    def set_row(k, row):
        row_of[pl.ds(k, 1), :] = lax.shift_right_arithmetic(row, 7)
        lane_hot[k] = jnp.where(matches(row & (LANES - 1), LANES), 1.0, 0.0).astype(jnp.bfloat16)

    @pl.loop(0, given)
    def _(k):
        set_row(k, idx[pl.ds(k, 1), :])

    before = (
        lax.broadcasted_iota(jnp.int32, (width, width), 0)
        < lax.broadcasted_iota(jnp.int32, (width, width), 1)
    )
    before = jnp.where(before, 1.0, 0.0).astype(jnp.bfloat16)
    carry = jnp.zeros((n, 1), jnp.float32)
    found = jnp.zeros((2 * slots, width), jnp.float32)
    for j in range(owner.shape[0]):
        target = owner[j : j + 1, :]
        mask = matches(target, n)
        hot = jnp.where(mask, 1.0, 0.0)
        earlier = jnp.dot(hot.astype(jnp.bfloat16), before, preferred_element_type=jnp.float32)
        rank = jnp.sum(jnp.where(mask, earlier + carry, 0.0), axis=0, keepdims=True)
        carry = carry + jnp.sum(hot, axis=1, keepdims=True)
        slot = target * cap + rank.astype(jnp.int32)
        mask = matches(lax.div(slot, width), slots)
        number = node[j : j + 1, :] + 1
        left = jnp.concatenate(
            [
                jnp.where(mask, lax.shift_right_arithmetic(number, 6).astype(jnp.float32), 0.0),
                jnp.where(mask, (number & 63).astype(jnp.float32), 0.0),
            ],
            axis=0,
        ).astype(jnp.bfloat16)
        right = jnp.where(matches(lax.rem(slot, width), width), 1.0, 0.0).astype(jnp.bfloat16)
        found = found + lax.dot_general(
            left, right, (((1,), (1,)), ((), ())), preferred_element_type=jnp.float32
        )
    numbers = (found[:slots] * 64.0 + found[slots:]).astype(jnp.int32) - 1
    for q in range(slots):
        set_row(given + q, numbers[q : q + 1, :])

    cur[...] = disp[...]
    old[...] = prev[...]
    ext[...] = jnp.zeros_like(ext)

    def box_copy(i, d):
        other = lax.rem(me + d, n)
        return pltpu.make_async_remote_copy(
            src_ref=box_out.at[i, other],
            dst_ref=box_in.at[i, me],
            send_sem=box_send.at[i],
            recv_sem=box_recv.at[i],
            device_id=place(other),
            device_id_type=MESH,
        )

    def box_start(i):
        @pl.loop(1, n)
        def _(d):
            box_copy(i, d).start()

        box_in[i, me] = box_out[i, me]

    def box_wait(i):
        every = pl.ds(0, n - 1)
        whole = pltpu.make_async_remote_copy(
            src_ref=box_out.at[i, every],
            dst_ref=box_in.at[i, every],
            send_sem=box_send.at[i],
            recv_sem=box_recv.at[i],
            device_id=place(lax.rem(me + 1, n)),
            device_id_type=MESH,
        )
        whole.wait()

    def halo_copies(i):
        copies = []
        for side, step in ((0, n - 1), (1, 1)):
            copies.append(
                pltpu.make_async_remote_copy(
                    src_ref=halo_out.at[i, side],
                    dst_ref=halo_in.at[i, 1 - side],
                    send_sem=halo_send.at[i, side],
                    recv_sem=halo_recv.at[i, 1 - side],
                    device_id=place(lax.rem(me + step, n)),
                    device_id_type=MESH,
                )
            )
        return copies

    def halo_start(i):
        for copy in halo_copies(i):
            copy.start()

    def halo_wait(i):
        for copy in halo_copies(i):
            copy.wait()

    def halo_side(i, side, c):
        inside = me > 0 if side == 0 else me < n - 1
        return jnp.where(inside, halo_in[i, side, c : c + 1, :], 0.0)

    lent_rows = lent // LANES

    for step in range(STEPS):
        going, back = 2 * step, 2 * step + 1
        own_tab[...] = side_by_side(cur[...])
        lending = gather(own_tab[...], lane_hot[lend], row_of[lend : lend + 1, :], own_rows)
        for c in range(3):
            for side in range(2):
                halo_out[going, side, c : c + 1, :] = lending[c][:, side * lent : (side + 1) * lent]
        if step == 0:
            pl.semaphore_wait(barrier, n - 1)
        halo_start(going)

        @pl.loop(0, slots)
        def _(q):
            k = given + q
            got = gather(own_tab[...], lane_hot[k], row_of[pl.ds(k, 1), :], own_rows)
            for c in range(3):
                slot_vals[c, pl.ds(q, 1), :] = got[c]

        for o in range(n):
            r, l = divmod(o * cap, width)
            for c in range(3):
                box_out[going, o, c : c + 1, :] = slot_vals[c, r : r + 1, l : l + cap]
        box_start(going)

        halo_wait(going)
        for c in range(3):
            ext[c * ext_rows : c * ext_rows + own_rows, :] = cur[c * own_rows : (c + 1) * own_rows, :]
            for side in range(2):
                ghosts = halo_side(going, side, c)
                for r in range(lent_rows):
                    at = c * ext_rows + own_rows + side * lent_rows + r
                    ext[at : at + 1, :] = ghosts[:, r * LANES : (r + 1) * LANES]
        ext_tab[...] = side_by_side(ext[...])

        @pl.loop(0, elnode)
        def _(k):
            got = gather(ext_tab[...], lane_hot[k], row_of[pl.ds(k, 1), :], ext_rows)
            for c in range(3):
                ue[pl.ds(c * elnode + k, 1), :] = got[c]

        box_wait(going)
        for g in range(n):
            r, l = divmod(g * cap, LANES)
            for c in range(3):
                at = c * slot_rows + r
                recv_tab[at : at + 1, l : l + cap] = box_in[going, g, c : c + 1, :]
        table = side_by_side(recv_tab[...])
        total = jnp.zeros((6 * slot_rows, LANES), jnp.float32)
        for p in range(pair_chunks):
            cols = slice(p * width, (p + 1) * width)
            near_rows, far_rows = row_of[near + p : near + p + 1, :], row_of[far + p : far + p + 1, :]
            low = gather(table, lane_hot[near + p], near_rows, slot_rows)
            high = gather(table, lane_hot[far + p], far_rows, slot_rows)
            gap = [gap0[c : c + 1, cols] + high[c] - low[c] for c in range(3)]
            normal = pen[:, cols] * jnp.maximum(-gap[2], 0.0)
            length = jnp.sqrt(gap[0] * gap[0] + gap[1] * gap[1] + 0.01)
            slipping = slip[step : step + 1, cols] == 1
            factor = jnp.where(
                slipping, -fric[:, cols] * normal / length, -0.5 * pen[:, cols]
            )
            force = [factor * gap[0], factor * gap[1], normal]
            total = total + scatter(force, lane_hot[far + p], far_rows, slot_rows)
            total = total - scatter(force, lane_hot[near + p], near_rows, slot_rows)
        pair_vals[...] = total[: 3 * slot_rows] + total[3 * slot_rows :]
        for g in range(n):
            r, l = divmod(g * cap, LANES)
            for c in range(3):
                at = c * slot_rows + r
                box_out[back, g, c : c + 1, :] = pair_vals[at : at + 1, l : l + cap]
        box_start(back)

        fe[...] = (
            jnp.dot(
                stiff[...],
                ue[...],
                precision=lax.Precision.HIGHEST,
                preferred_element_type=jnp.float32,
            )
            * mod[...]
        )
        acc_e[...] = jnp.zeros_like(acc_e)

        @pl.loop(0, elnode)
        def _(k):
            values = [fe[pl.ds(c * elnode + k, 1), :] for c in range(3)]
            acc_e[...] += scatter(values, lane_hot[k], row_of[pl.ds(k, 1), :], ext_rows)

        ext[...] = acc_e[: 3 * ext_rows] + acc_e[3 * ext_rows :]
        for c in range(3):
            for side in range(2):
                for r in range(lent_rows):
                    at = c * ext_rows + own_rows + side * lent_rows + r
                    halo_out[back, side, c : c + 1, r * LANES : (r + 1) * LANES] = ext[at : at + 1, :]
        halo_start(back)

        box_wait(back)
        for o in range(n):
            r, l = divmod(o * cap, width)
            for c in range(3):
                slot_vals[c, r : r + 1, l : l + cap] = box_in[back, o, c : c + 1, :]
        acc_c[...] = jnp.zeros_like(acc_c)

        @pl.loop(0, slots)
        def _(q):
            k = given + q
            values = [slot_vals[c, pl.ds(q, 1), :] for c in range(3)]
            acc_c[...] += scatter(values, lane_hot[k], row_of[pl.ds(k, 1), :], own_rows)

        halo_wait(back)
        values = [
            jnp.concatenate([halo_side(back, 0, c), halo_side(back, 1, c)], axis=1) for c in range(3)
        ]
        ghost = scatter(values, lane_hot[lend], row_of[lend : lend + 1, :], own_rows)
        total = acc_c[...] - ghost
        total = total[: 3 * own_rows] + total[3 * own_rows :]
        for c in range(3):
            rows = slice(c * own_rows, (c + 1) * own_rows)
            internal = ext[c * ext_rows : c * ext_rows + own_rows, :]
            acceleration = (load[rows, :] - internal + total[rows]) / mass[...]
            now = cur[rows, :]
            later = 2.0 * now - old[rows, :] + time_step_sq * acceleration
            old[rows, :] = now
            cur[rows, :] = later
            if step == STEPS - 1:
                out_u[rows, :] = later
                out_a[rows, :] = acceleration


def on_device(
    n_py,
    displacement,
    disp_prev,
    nodal_load,
    nodal_mass,
    modulus,
    stiffness,
    connectivity,
    ghost_send,
    contact_node,
    contact_owner,
    pair_ids,
    gap_start,
    penalty,
    friction,
    slip_state,
):
    n = lax.axis_size(("px", "py"))
    cap = 2 * contact_node.shape[0] // n
    elnode, width = connectivity.shape
    nodes = displacement.shape[1]
    lent = ghost_send.shape[1]
    own_rows = nodes // LANES
    ext_rows = -(-(own_rows + 2 * lent // LANES) // SUBLANES) * SUBLANES
    slots = n * cap // width
    slot_rows = n * cap // LANES
    idx = jnp.concatenate(
        [connectivity, ghost_send.reshape(1, 2 * lent), pair_ids.reshape(-1, width)], axis=0
    )
    chunks = idx.shape[0] + slots
    flat = (3 * own_rows, LANES)
    vmem = pl.BlockSpec(memory_space=pltpu.VMEM)
    f32, bf16 = jnp.float32, jnp.bfloat16
    dma = pltpu.SemaphoreType.DMA
    new_u, acc = pl.pallas_call(
        functools.partial(kernel, (n_py, n, cap, elnode, lent, width)),
        out_shape=[jax.ShapeDtypeStruct(flat, f32)] * 2,
        in_specs=[vmem] * 13,
        out_specs=[vmem] * 2,
        scratch_shapes=[
            pltpu.VMEM((chunks, width), jnp.int32),
            pltpu.VMEM((chunks, LANES, width), bf16),
            pltpu.VMEM((3 * own_rows, 2 * LANES), bf16),
            pltpu.VMEM((3 * ext_rows, LANES), f32),
            pltpu.VMEM((3 * ext_rows, 2 * LANES), bf16),
            pltpu.VMEM((3 * elnode, width), f32),
            pltpu.VMEM((3 * elnode, width), f32),
            pltpu.VMEM((6 * ext_rows, LANES), f32),
            pltpu.VMEM((6 * own_rows, LANES), f32),
            pltpu.VMEM((3, slots, width), f32),
            pltpu.VMEM((3 * slot_rows, LANES), f32),
            pltpu.VMEM((3 * slot_rows, LANES), f32),
            pltpu.VMEM(flat, f32),
            pltpu.VMEM(flat, f32),
            pltpu.VMEM((2 * STEPS, n, 3, cap), f32),
            pltpu.VMEM((2 * STEPS, n, 3, cap), f32),
            pltpu.VMEM((2 * STEPS, 2, 3, lent), f32),
            pltpu.VMEM((2 * STEPS, 2, 3, lent), f32),
            dma((2 * STEPS,)),
            dma((2 * STEPS,)),
            dma((2 * STEPS, 2)),
            dma((2 * STEPS, 2)),
        ],
        compiler_params=pltpu.CompilerParams(
            collective_id=0, has_side_effects=True, vmem_limit_bytes=48 * 1024 * 1024
        ),
        name="contact_steps",
    )(
        idx,
        contact_owner.reshape(-1, width),
        contact_node.reshape(-1, width),
        modulus.reshape(1, -1),
        stiffness,
        gap_start,
        penalty.reshape(1, -1),
        friction.reshape(1, -1),
        slip_state,
        displacement.reshape(flat),
        disp_prev.reshape(flat),
        nodal_load.reshape(flat),
        nodal_mass.reshape(-1, LANES),
    )
    return new_u.reshape(displacement.shape), acc.reshape(displacement.shape)


def solution(mesh):
    both = ("px", "py")
    row, cols = P(both), P(None, both)
    return jax.shard_map(
        functools.partial(on_device, mesh.shape["py"]),
        mesh=mesh,
        in_specs=(cols, cols, cols, row, row, P(), cols, cols, row, row, cols, cols, row, row, cols),
        out_specs=(cols, cols),
        check_vma=False,
    )
```

profile of v0, /device:TPU:0, one launch (start us, length us, event | category | flops | bytes accessed | tf_op | source)
XLA Modules:
  0.0 79.9 jit_solution(2102461163058481858)
XLA Ops:
  0.6 0.0 copy-start.10
  0.6 0.7 copy.17
  1.3 0.0 copy-done.10
  1.3 0.0 copy-start.11
  1.3 0.7 copy-done.11
  2.0 0.0 copy-start.12
  2.0 0.7 copy-done.12
  2.7 0.0 copy-start.7
  2.7 0.9 %reshape.50.disp = f32[96,128]{1,0:T(8,128)S(1)} reshape(f32[3,4096]{1,0:T(4,128)} %param.15) | data formatting | bytes 98304 | tf_op jit(solution)/shard_map/reshape | solution.py:429
  3.7 0.0 copy-done.7
  3.7 0.0 copy-start.8
  3.7 0.8 copy-done.8
  4.5 0.0 copy-start.9
  4.6 0.8 copy-done.9
  5.4 0.0 copy-start
  5.4 0.0 copy-start.1
  5.4 0.0 copy-start.2
  5.4 0.0 copy-start.3
  5.4 0.0 copy-start.4
  5.4 0.0 copy-start.5
  5.4 0.0 copy-start.6
  5.4 0.7 copy-done
  6.1 0.0 copy-done.1
  6.1 0.0 copy-done.2
  6.1 0.0 copy-done.3
  6.1 0.0 copy-done.4
  6.2 0.0 copy-done.5
  6.2 0.0 copy-done.6
  6.2 72.4 %contact_steps.1 = (f32[96,128]{1,0:T(8,128)S(1)}, f32[96,128]{1,0:T(8,128)S(1)}) custom-call(s32[32,512]{1,0:T(8,128)S(1)} %pad_add_fusion.idx, s32[4,512]{1,0:T(4,128)S(1)} %reshape.45.owner, s32[4,512]{1,0:T(4,128)S(1)} %reshape.46.node, f32[1,512]{1,0:T(1,128)S(1)} %bitcast.10, f32[81,81]{1,0:T(8,128)S(1)} %copy-done, f32[3,1024]{1,0:T(4,128)S(1)} %copy-done.1, ...), custom_call_target="tpu_custom_call" | custom-call | tf_op jit(solution)/shard_map/contact_steps/pallas_call | solution.py:386
  78.6 0.7 reshape.54
  79.3 0.7 reshape.55
  (6 shorter events, 0.1 us)
Async XLA Ops:
  0.6 0.7 copy-start.10
  1.3 0.7 copy-start.11
  2.0 0.7 copy-start.12
  2.7 0.9 %copy-start.7 = (f32[3,4096]{1,0:T(4,128)S(1)}, f32[3,4096]{1,0:T(4,128)}, u32[]{:S(2)}) copy-start(f32[3,4096]{1,0:T(4,128)} %param.16) | copy-start | bytes 147460
  3.7 0.8 %copy-start.8 = (f32[3,4096]{1,0:T(4,128)S(1)}, f32[3,4096]{1,0:T(4,128)}, u32[]{:S(2)}) copy-start(f32[3,4096]{1,0:T(4,128)} %param.17) | copy-start | bytes 147460
  4.5 0.8 %copy-start.9 = (s32[27,512]{1,0:T(8,128)S(1)}, s32[27,512]{1,0:T(8,128)}, u32[]{:S(2)}) copy-start(s32[27,512]{1,0:T(8,128)} %param.21) | copy-start | bytes 165892
  5.4 0.8 copy-start
  5.4 0.8 copy-start.1
  5.4 0.8 copy-start.2
  5.4 0.8 copy-start.3
  5.4 0.8 copy-start.4
  5.4 0.8 copy-start.5
  5.4 0.8 copy-start.6
where the time goes:
time: 80.3 us; the launch traced here: 79.9 us
  Pallas kernels  72.4 us (90%)
  local copies, waits for them, and re-layouts  6.73 us (8%)
    pallas_call x1, Pallas kernels, on_device(): pl.pallas_call(functools.partial(kernel, (n_py, n, cap, elnode, lent, wid...  72.4 us
    unnamed x27, local copies, waits for them, and re-layouts  4.41 us

commit v1 on v0

--- a/solution.py
+++ b/solution.py
@@ -24,21 +24,21 @@
     return high, (value - high.astype(jnp.float32)).astype(jnp.bfloat16)
 
 
-def side_by_side(table):
-    return jnp.concatenate(split(table), axis=1)
-
-
-def gather(table, lane_hot, row_index, rows):
-    got = jnp.dot(
-        table,
-        jnp.concatenate([lane_hot, lane_hot], axis=0),
-        preferred_element_type=jnp.float32,
-    )
-    mask = matches(row_index, rows)
-    return [
-        jnp.sum(jnp.where(mask, got[c * rows : (c + 1) * rows], 0.0), axis=0, keepdims=True)
-        for c in range(3)
-    ]
+def gather(table, idx, start, rows):
+    width = idx.shape[1]
+    blocks = [idx[pl.ds(start, SUBLANES), l : l + LANES] for l in range(0, width, LANES)]
+    row_of = [lax.shift_right_arithmetic(block, 7) for block in blocks]
+    lane_of = [block & (LANES - 1) for block in blocks]
+    got = [[jnp.zeros((SUBLANES, LANES), jnp.float32)] * len(blocks) for _ in range(3)]
+    for r in range(rows):
+        masks = [row == r for row in row_of]
+        for c in range(3):
+            at = c * rows + r
+            line = jnp.broadcast_to(table[at : at + 1, :], (SUBLANES, LANES))
+            for b, lane in enumerate(lane_of):
+                value = jnp.take_along_axis(line, lane, axis=1, mode="promise_in_bounds")
+                got[c][b] = jnp.where(masks[b], value, got[c][b])
+    return [jnp.concatenate(parts, axis=1) for parts in got]
 
 
 def scatter(values, lane_hot, row_index, rows):
@@ -55,7 +55,7 @@
 
 def kernel(
     dims,
-    idx,
+    given_idx,
     owner,
     node,
     mod,
@@ -70,15 +70,13 @@
     mass,
     out_u,
     out_a,
-    row_of,
+    idx,
     lane_hot,
-    own_tab,
+    stiff_wide,
     ext,
-    ext_tab,
     ue,
     fe,
     acc_e,
-    acc_c,
     slot_vals,
     pair_vals,
     recv_tab,
@@ -112,18 +110,30 @@
     ext_rows = ext.shape[0] // 3
     slots = slot_vals.shape[1]
     slot_rows = recv_tab.shape[0] // 3
-    given = idx.shape[0]
-    lend = elnode
+    given = given_idx.shape[0]
+    wide = stiff_wide.shape[0] // 3
+    lend = wide
     pair_chunks = pen.shape[1] // width
-    near, far = elnode + 1, elnode + 1 + pair_chunks
+    near, far = lend + 1, lend + 1 + pair_chunks
 
     def set_row(k, row):
-        row_of[pl.ds(k, 1), :] = lax.shift_right_arithmetic(row, 7)
+        idx[pl.ds(k, 1), :] = row
         lane_hot[k] = jnp.where(matches(row & (LANES - 1), LANES), 1.0, 0.0).astype(jnp.bfloat16)
+
+    def scatter_row(values, k, rows):
+        row = lax.shift_right_arithmetic(idx[pl.ds(k, 1), :], 7)
+        return scatter(values, lane_hot[k], row, rows)
 
     @pl.loop(0, given)
     def _(k):
-        set_row(k, idx[pl.ds(k, 1), :])
+        set_row(k, given_idx[pl.ds(k, 1), :])
+
+    stiff_wide[...] = jnp.zeros_like(stiff_wide)
+    for c in range(3):
+        for d in range(3):
+            stiff_wide[c * wide : c * wide + elnode, d * wide : d * wide + elnode] = stiff[
+                c * elnode : (c + 1) * elnode, d * elnode : (d + 1) * elnode
+            ]
 
     before = (
         lax.broadcasted_iota(jnp.int32, (width, width), 0)
@@ -222,8 +232,7 @@
 
     for step in range(STEPS):
         going, back = 2 * step, 2 * step + 1
-        own_tab[...] = side_by_side(cur[...])
-        lending = gather(own_tab[...], lane_hot[lend], row_of[lend : lend + 1, :], own_rows)
+        lending = [value[:1] for value in gather(cur, idx, lend, own_rows)]
         for c in range(3):
             for side in range(2):
                 halo_out[going, side, c : c + 1, :] = lending[c][:, side * lent : (side + 1) * lent]
@@ -231,12 +240,10 @@
             pl.semaphore_wait(barrier, n - 1)
         halo_start(going)
 
-        @pl.loop(0, slots)
-        def _(q):
-            k = given + q
-            got = gather(own_tab[...], lane_hot[k], row_of[pl.ds(k, 1), :], own_rows)
-            for c in range(3):
-                slot_vals[c, pl.ds(q, 1), :] = got[c]
+        for q in range(0, slots, SUBLANES):
+            got = gather(cur, idx, given + q, own_rows)
+            for c in range(3):
+                slot_vals[c, q : q + SUBLANES, :] = got[c]
 
         for o in range(n):
             r, l = divmod(o * cap, width)
@@ -252,13 +259,13 @@
                 for r in range(lent_rows):
                     at = c * ext_rows + own_rows + side * lent_rows + r
                     ext[at : at + 1, :] = ghosts[:, r * LANES : (r + 1) * LANES]
-        ext_tab[...] = side_by_side(ext[...])
-
-        @pl.loop(0, elnode)
-        def _(k):
-            got = gather(ext_tab[...], lane_hot[k], row_of[pl.ds(k, 1), :], ext_rows)
-            for c in range(3):
-                ue[pl.ds(c * elnode + k, 1), :] = got[c]
+
+        @pl.loop(0, wide // SUBLANES)
+        def _(group):
+            start = pl.multiple_of(group * SUBLANES, SUBLANES)
+            got = gather(ext, idx, start, ext_rows)
+            for c in range(3):
+                ue[pl.ds(pl.multiple_of(c * wide + start, SUBLANES), SUBLANES), :] = got[c]
 
         box_wait(going)
         for g in range(n):
@@ -266,13 +273,12 @@
             for c in range(3):
                 at = c * slot_rows + r
                 recv_tab[at : at + 1, l : l + cap] = box_in[going, g, c : c + 1, :]
-        table = side_by_side(recv_tab[...])
+        ends = gather(recv_tab, idx, lend, slot_rows)
         total = jnp.zeros((6 * slot_rows, LANES), jnp.float32)
         for p in range(pair_chunks):
             cols = slice(p * width, (p + 1) * width)
-            near_rows, far_rows = row_of[near + p : near + p + 1, :], row_of[far + p : far + p + 1, :]
-            low = gather(table, lane_hot[near + p], near_rows, slot_rows)
-            high = gather(table, lane_hot[far + p], far_rows, slot_rows)
+            low = [value[1 + p : 2 + p] for value in ends]
+            high = [value[1 + pair_chunks + p : 2 + pair_chunks + p] for value in ends]
             gap = [gap0[c : c + 1, cols] + high[c] - low[c] for c in range(3)]
             normal = pen[:, cols] * jnp.maximum(-gap[2], 0.0)
             length = jnp.sqrt(gap[0] * gap[0] + gap[1] * gap[1] + 0.01)
@@ -281,8 +287,8 @@
                 slipping, -fric[:, cols] * normal / length, -0.5 * pen[:, cols]
             )
             force = [factor * gap[0], factor * gap[1], normal]
-            total = total + scatter(force, lane_hot[far + p], far_rows, slot_rows)
-            total = total - scatter(force, lane_hot[near + p], near_rows, slot_rows)
+            total = total + scatter_row(force, far + p, slot_rows)
+            total = total - scatter_row(force, near + p, slot_rows)
         pair_vals[...] = total[: 3 * slot_rows] + total[3 * slot_rows :]
         for g in range(n):
             r, l = divmod(g * cap, LANES)
@@ -293,7 +299,7 @@
 
         fe[...] = (
             jnp.dot(
-                stiff[...],
+                stiff_wide[...],
                 ue[...],
                 precision=lax.Precision.HIGHEST,
                 preferred_element_type=jnp.float32,
@@ -302,10 +308,16 @@
         )
         acc_e[...] = jnp.zeros_like(acc_e)
 
-        @pl.loop(0, elnode)
-        def _(k):
-            values = [fe[pl.ds(c * elnode + k, 1), :] for c in range(3)]
-            acc_e[...] += scatter(values, lane_hot[k], row_of[pl.ds(k, 1), :], ext_rows)
+        some = next(f for f in (9, 3, 1) if elnode % f == 0)
+
+        @pl.loop(0, elnode // some)
+        def _(group):
+            total = acc_e[...]
+            for i in range(some):
+                k = group * some + i
+                values = [fe[pl.ds(c * wide + k, 1), :] for c in range(3)]
+                total = total + scatter_row(values, k, ext_rows)
+            acc_e[...] = total
 
         ext[...] = acc_e[: 3 * ext_rows] + acc_e[3 * ext_rows :]
         for c in range(3):
@@ -320,20 +332,16 @@
             r, l = divmod(o * cap, width)
             for c in range(3):
                 slot_vals[c, r : r + 1, l : l + cap] = box_in[back, o, c : c + 1, :]
-        acc_c[...] = jnp.zeros_like(acc_c)
-
-        @pl.loop(0, slots)
-        def _(q):
-            k = given + q
-            values = [slot_vals[c, pl.ds(q, 1), :] for c in range(3)]
-            acc_c[...] += scatter(values, lane_hot[k], row_of[pl.ds(k, 1), :], own_rows)
+        contact = jnp.zeros((6 * own_rows, LANES), jnp.float32)
+        for q in range(slots):
+            values = [slot_vals[c, q : q + 1, :] for c in range(3)]
+            contact = contact + scatter_row(values, given + q, own_rows)
 
         halo_wait(back)
         values = [
             jnp.concatenate([halo_side(back, 0, c), halo_side(back, 1, c)], axis=1) for c in range(3)
         ]
-        ghost = scatter(values, lane_hot[lend], row_of[lend : lend + 1, :], own_rows)
-        total = acc_c[...] - ghost
+        total = contact - scatter_row(values, lend, own_rows)
         total = total[: 3 * own_rows] + total[3 * own_rows :]
         for c in range(3):
             rows = slice(c * own_rows, (c + 1) * own_rows)
@@ -375,8 +383,15 @@
     ext_rows = -(-(own_rows + 2 * lent // LANES) // SUBLANES) * SUBLANES
     slots = n * cap // width
     slot_rows = n * cap // LANES
+    wide = -(-elnode // SUBLANES) * SUBLANES
+    pairs = pair_ids.reshape(-1, width)
     idx = jnp.concatenate(
-        [connectivity, ghost_send.reshape(1, 2 * lent), pair_ids.reshape(-1, width)], axis=0
+        [
+            jnp.pad(connectivity, ((0, wide - elnode), (0, 0)), constant_values=-1),
+            ghost_send.reshape(1, 2 * lent),
+            jnp.pad(pairs, ((0, -(1 + pairs.shape[0]) % SUBLANES), (0, 0)), constant_values=-1),
+        ],
+        axis=0,
     )
     chunks = idx.shape[0] + slots
     flat = (3 * own_rows, LANES)
@@ -391,13 +406,11 @@
         scratch_shapes=[
             pltpu.VMEM((chunks, width), jnp.int32),
             pltpu.VMEM((chunks, LANES, width), bf16),
-            pltpu.VMEM((3 * own_rows, 2 * LANES), bf16),
+            pltpu.VMEM((3 * wide, 3 * wide), f32),
             pltpu.VMEM((3 * ext_rows, LANES), f32),
-            pltpu.VMEM((3 * ext_rows, 2 * LANES), bf16),
-            pltpu.VMEM((3 * elnode, width), f32),
-            pltpu.VMEM((3 * elnode, width), f32),
+            pltpu.VMEM((3 * wide, width), f32),
+            pltpu.VMEM((3 * wide, width), f32),
             pltpu.VMEM((6 * ext_rows, LANES), f32),
-            pltpu.VMEM((6 * own_rows, LANES), f32),
             pltpu.VMEM((3, slots, width), f32),
             pltpu.VMEM((3 * slot_rows, LANES), f32),
             pltpu.VMEM((3 * slot_rows, LANES), f32),

time: 80.3 us -> 73.9 us (0.920)
  Pallas kernels: 72.4 us -> 66 us
    pallas_call x1, Pallas kernels: 72.4 us -> 66 us  [on_device(): pl.pallas_call(functools.partial(kernel, (n_py, n, cap, elnode, lent, wid...]
where the time goes in v1:
time: 73.9 us; the launch traced here: 73.4 us
  Pallas kernels  66 us (89%)
  local copies, waits for them, and re-layouts  6.73 us (9%)
  between operations  0.74 us (1%)
    pallas_call x1, Pallas kernels, on_device(): pl.pallas_call(functools.partial(kernel, (n_py, n, cap, elnode, lent, wid...  66 us
    unnamed x27, local copies, waits for them, and re-layouts  4.41 us

profile of v1, /device:TPU:0, one launch (start us, length us, event | category | flops | bytes accessed | tf_op | source)
XLA Modules:
  0.0 73.4 jit_solution(5703063219228688943)
XLA Ops:
  0.6 0.0 copy-start.10
  0.6 0.7 copy.17
  1.3 0.0 copy-done.10
  1.3 0.0 copy-start.11
  1.3 0.7 copy-done.11
  2.0 0.0 copy-start.12
  2.0 0.7 copy-done.12
  2.7 0.0 copy-start.7
  2.7 0.9 %reshape.50.disp = f32[96,128]{1,0:T(8,128)S(1)} reshape(f32[3,4096]{1,0:T(4,128)} %param.15) | data formatting | bytes 98304 | tf_op jit(solution)/shard_map/reshape | solution.py:442
  3.7 0.0 copy-done.7
  3.7 0.0 copy-start.8
  3.7 0.8 %copy-done.8 = f32[3,4096]{1,0:T(4,128)S(1)} copy-done((f32[3,4096]{1,0:T(4,128)S(1)}, f32[3,4096]{1,0:T(4,128)}, u32[]{:S(2)}) %copy-start.8) | copy-done | bytes 49176
  4.5 0.0 copy-start.9
  4.6 0.8 %copy-done.9 = s32[27,512]{1,0:T(8,128)S(1)} copy-done((s32[27,512]{1,0:T(8,128)S(1)}, s32[27,512]{1,0:T(8,128)}, u32[]{:S(2)}) %copy-start.9) | copy-done | bytes 55320
  5.4 0.0 copy-start
  5.4 0.0 copy-start.1
  5.4 0.0 copy-start.2
  5.4 0.0 copy-start.3
  5.4 0.0 copy-start.4
  5.4 0.0 copy-start.5
  5.4 0.0 copy-start.6
  5.4 0.7 copy-done
  6.1 0.0 copy-done.1
  6.1 0.0 copy-done.2
  6.1 0.0 copy-done.3
  6.1 0.0 copy-done.4
  6.2 0.0 copy-done.5
  6.2 0.0 copy-done.6
  6.2 66.0 %contact_steps.1 = (f32[96,128]{1,0:T(8,128)S(1)}, f32[96,128]{1,0:T(8,128)S(1)}) custom-call(s32[40,512]{1,0:T(8,128)S(1)} %select_add_fusion.given_idx, s32[4,512]{1,0:T(4,128)S(1)} %reshape.45.owner, s32[4,512]{1,0:T(4,128)S(1)} %reshape.46.node, f32[1,512]{1,0:T(1,128)S(1)} %bitcast.10, f32[81,81]{1,0:T(8,128)S(1)} %copy-done, f32[3,1024]{1,0:T(4,128)S(1)} %copy-done.1, ...), custom_call_target="tpu_custom_call" | custom-call | tf_op jit(solution)/shard_map/contact_steps/pallas_call | solution.py:401
  72.1 0.7 reshape.54
  72.8 0.7 reshape.55
  (6 shorter events, 0.1 us)
Async XLA Ops:
  0.6 0.7 copy-start.10
  1.3 0.7 copy-start.11
  2.0 0.7 copy-start.12
  2.7 0.9 %copy-start.7 = (f32[3,4096]{1,0:T(4,128)S(1)}, f32[3,4096]{1,0:T(4,128)}, u32[]{:S(2)}) copy-start(f32[3,4096]{1,0:T(4,128)} %param.16) | copy-start | bytes 147460
  3.7 0.8 %copy-start.8 = (f32[3,4096]{1,0:T(4,128)S(1)}, f32[3,4096]{1,0:T(4,128)}, u32[]{:S(2)}) copy-start(f32[3,4096]{1,0:T(4,128)} %param.17) | copy-start | bytes 147460
  4.5 0.8 %copy-start.9 = (s32[27,512]{1,0:T(8,128)S(1)}, s32[27,512]{1,0:T(8,128)}, u32[]{:S(2)}) copy-start(s32[27,512]{1,0:T(8,128)} %param.21) | copy-start | bytes 165892
  5.4 0.8 %copy-start = (f32[81,81]{1,0:T(8,128)S(1)}, f32[81,81]{1,0:T(8,128)}, u32[]{:S(2)}) copy-start(f32[81,81]{1,0:T(8,128)} %stiff.1) | copy-start | bytes 78736
  5.4 0.8 %copy-start.1 = (f32[3,1024]{1,0:T(4,128)S(1)}, f32[3,1024]{1,0:T(4,128)}, u32[]{:S(2)}) copy-start(f32[3,1024]{1,0:T(4,128)} %gap0.1) | copy-start | bytes 36868
  5.4 0.8 %copy-start.2 = (s32[3,1024]{1,0:T(4,128)S(1)}, s32[3,1024]{1,0:T(4,128)}, u32[]{:S(2)}) copy-start(s32[3,1024]{1,0:T(4,128)} %slip.1) | copy-start | bytes 36868
  5.4 0.8 %copy-start.3 = (f32[4096]{0:T(1024)S(1)}, f32[4096]{0:T(1024)}, u32[]{:S(2)}) copy-start(f32[4096]{0:T(1024)} %param.18) | copy-start | bytes 49156
  5.4 0.8 %copy-start.4 = (f32[1024]{0:T(1024)S(1)}, f32[1024]{0:T(1024)}, u32[]{:S(2)}) copy-start(f32[1024]{0:T(1024)} %param.27) | copy-start | bytes 12292
  5.4 0.8 %copy-start.5 = (f32[1024]{0:T(1024)S(1)}, f32[1024]{0:T(1024)}, u32[]{:S(2)}) copy-start(f32[1024]{0:T(1024)} %param.28) | copy-start | bytes 12292
  5.4 0.8 %copy-start.6 = (f32[512]{0:T(512)S(1)}, f32[512]{0:T(512)}, u32[]{:S(2)}) copy-start(f32[512]{0:T(512)} %param.19) | copy-start | bytes 6148

commit v2 on v1

--- a/solution.py
+++ b/solution.py
@@ -24,21 +24,18 @@
     return high, (value - high.astype(jnp.float32)).astype(jnp.bfloat16)
 
 
-def gather(table, idx, start, rows):
-    width = idx.shape[1]
-    blocks = [idx[pl.ds(start, SUBLANES), l : l + LANES] for l in range(0, width, LANES)]
-    row_of = [lax.shift_right_arithmetic(block, 7) for block in blocks]
-    lane_of = [block & (LANES - 1) for block in blocks]
-    got = [[jnp.zeros((SUBLANES, LANES), jnp.float32)] * len(blocks) for _ in range(3)]
-    for r in range(rows):
-        masks = [row == r for row in row_of]
+def gather_block(table, index, rows, used):
+    row_of = lax.shift_right_arithmetic(index, 7)
+    lane_of = index & (LANES - 1)
+    got = [jnp.zeros((SUBLANES, LANES), jnp.float32)] * 3
+    for r in range(used):
+        mask = row_of == r
         for c in range(3):
             at = c * rows + r
             line = jnp.broadcast_to(table[at : at + 1, :], (SUBLANES, LANES))
-            for b, lane in enumerate(lane_of):
-                value = jnp.take_along_axis(line, lane, axis=1, mode="promise_in_bounds")
-                got[c][b] = jnp.where(masks[b], value, got[c][b])
-    return [jnp.concatenate(parts, axis=1) for parts in got]
+            value = jnp.take_along_axis(line, lane_of, axis=1, mode="promise_in_bounds")
+            got[c] = jnp.where(mask, value, got[c])
+    return got
 
 
 def scatter(values, lane_hot, row_index, rows):
@@ -56,6 +53,7 @@
 def kernel(
     dims,
     given_idx,
+    lend_idx,
     owner,
     node,
     mod,
@@ -78,6 +76,7 @@
     fe,
     acc_e,
     slot_vals,
+    ends,
     pair_vals,
     recv_tab,
     cur,
@@ -229,21 +228,41 @@
         return jnp.where(inside, halo_in[i, side, c : c + 1, :], 0.0)
 
     lent_rows = lent // LANES
+    blocks = width // LANES
+
+    def gather_rows(table, first, count, rows, used, store):
+        @pl.loop(0, count // SUBLANES * blocks, unroll=2)
+        def _(i):
+            row = pl.multiple_of(lax.div(i, blocks) * SUBLANES, SUBLANES)
+            lane = pl.multiple_of(lax.rem(i, blocks) * LANES, LANES)
+            index = idx[pl.ds(first + row, SUBLANES), pl.ds(lane, LANES)]
+            for c, value in enumerate(gather_block(table, index, rows, used)):
+                store(c, pl.ds(row, SUBLANES), pl.ds(lane, LANES), value)
+
+    def slot_store(c, rows, lanes, value):
+        slot_vals[c, rows, lanes] = value
+
+    def element_store(c, rows, lanes, value):
+        ue[c, rows, lanes] = value
+
+    def end_store(c, rows, lanes, value):
+        ends[c, rows, lanes] = value
 
     for step in range(STEPS):
         going, back = 2 * step, 2 * step + 1
-        lending = [value[:1] for value in gather(cur, idx, lend, own_rows)]
+        lending = gather_block(cur, lend_idx[...], own_rows, own_rows)
         for c in range(3):
             for side in range(2):
-                halo_out[going, side, c : c + 1, :] = lending[c][:, side * lent : (side + 1) * lent]
+                for r in range(lent_rows):
+                    at = side * lent_rows + r
+                    halo_out[going, side, c : c + 1, r * LANES : (r + 1) * LANES] = lending[c][
+                        at : at + 1
+                    ]
         if step == 0:
             pl.semaphore_wait(barrier, n - 1)
         halo_start(going)
 
-        for q in range(0, slots, SUBLANES):
-            got = gather(cur, idx, given + q, own_rows)
-            for c in range(3):
-                slot_vals[c, q : q + SUBLANES, :] = got[c]
+        gather_rows(cur, given, slots, own_rows, own_rows, slot_store)
 
         for o in range(n):
             r, l = divmod(o * cap, width)
@@ -260,12 +279,7 @@
                     at = c * ext_rows + own_rows + side * lent_rows + r
                     ext[at : at + 1, :] = ghosts[:, r * LANES : (r + 1) * LANES]
 
-        @pl.loop(0, wide // SUBLANES)
-        def _(group):
-            start = pl.multiple_of(group * SUBLANES, SUBLANES)
-            got = gather(ext, idx, start, ext_rows)
-            for c in range(3):
-                ue[pl.ds(pl.multiple_of(c * wide + start, SUBLANES), SUBLANES), :] = got[c]
+        gather_rows(ext, 0, wide, ext_rows, own_rows + 2 * lent_rows, element_store)
 
         box_wait(going)
         for g in range(n):
@@ -273,12 +287,12 @@
             for c in range(3):
                 at = c * slot_rows + r
                 recv_tab[at : at + 1, l : l + cap] = box_in[going, g, c : c + 1, :]
-        ends = gather(recv_tab, idx, lend, slot_rows)
+        gather_rows(recv_tab, lend, SUBLANES, slot_rows, slot_rows, end_store)
         total = jnp.zeros((6 * slot_rows, LANES), jnp.float32)
         for p in range(pair_chunks):
             cols = slice(p * width, (p + 1) * width)
-            low = [value[1 + p : 2 + p] for value in ends]
-            high = [value[1 + pair_chunks + p : 2 + pair_chunks + p] for value in ends]
+            low = [ends[c, 1 + p : 2 + p, :] for c in range(3)]
+            high = [ends[c, 1 + pair_chunks + p : 2 + pair_chunks + p, :] for c in range(3)]
             gap = [gap0[c : c + 1, cols] + high[c] - low[c] for c in range(3)]
             normal = pen[:, cols] * jnp.maximum(-gap[2], 0.0)
             length = jnp.sqrt(gap[0] * gap[0] + gap[1] * gap[1] + 0.01)
@@ -300,7 +314,7 @@
         fe[...] = (
             jnp.dot(
                 stiff_wide[...],
-                ue[...],
+                ue[...].reshape(3 * wide, width),
                 precision=lax.Precision.HIGHEST,
                 preferred_element_type=jnp.float32,
             )
@@ -393,6 +407,8 @@
         ],
         axis=0,
     )
+    lend_idx = ghost_send.reshape(-1, LANES)
+    lend_idx = jnp.pad(lend_idx, ((0, -lend_idx.shape[0] % SUBLANES), (0, 0)), constant_values=-1)
     chunks = idx.shape[0] + slots
     flat = (3 * own_rows, LANES)
     vmem = pl.BlockSpec(memory_space=pltpu.VMEM)
@@ -401,17 +417,18 @@
     new_u, acc = pl.pallas_call(
         functools.partial(kernel, (n_py, n, cap, elnode, lent, width)),
         out_shape=[jax.ShapeDtypeStruct(flat, f32)] * 2,
-        in_specs=[vmem] * 13,
+        in_specs=[vmem] * 14,
         out_specs=[vmem] * 2,
         scratch_shapes=[
             pltpu.VMEM((chunks, width), jnp.int32),
             pltpu.VMEM((chunks, LANES, width), bf16),
             pltpu.VMEM((3 * wide, 3 * wide), f32),
             pltpu.VMEM((3 * ext_rows, LANES), f32),
-            pltpu.VMEM((3 * wide, width), f32),
+            pltpu.VMEM((3, wide, width), f32),
             pltpu.VMEM((3 * wide, width), f32),
             pltpu.VMEM((6 * ext_rows, LANES), f32),
             pltpu.VMEM((3, slots, width), f32),
+            pltpu.VMEM((3, SUBLANES, width), f32),
             pltpu.VMEM((3 * slot_rows, LANES), f32),
             pltpu.VMEM((3 * slot_rows, LANES), f32),
             pltpu.VMEM(flat, f32),
@@ -431,6 +448,7 @@
         name="contact_steps",
     )(
         idx,
+        lend_idx,
         contact_owner.reshape(-1, width),
         contact_node.reshape(-1, width),
         modulus.reshape(1, -1),

time: 73.9 us -> 60.8 us (0.82)
  Pallas kernels: 66 us -> 52.3 us
    pallas_call x1, Pallas kernels: 66 us -> 52.3 us  [on_device(): pl.pallas_call(functools.partial(kernel, (n_py, n, cap, elnode, lent, wid...]
    unnamed x27 -> x23, local copies, waits for them, and re-layouts: 4.41 us -> 3.11 us
    reshape x1, local copies, waits for them, and re-layouts: 0.91 us -> 0.04 us  [on_device(): displacement.reshape(flat)]
where the time goes in v2:
time: 60.8 us; the launch traced here: 60.4 us
  Pallas kernels  52.3 us (86%)
  local copies, waits for them, and re-layouts  7.38 us (12%)
  between operations  0.73 us (1%)
    pallas_call x1, Pallas kernels, on_device(): pl.pallas_call(functools.partial(kernel, (n_py, n, cap, elnode, lent, wid...  52.3 us
    unnamed x23, local copies, waits for them, and re-layouts  3.11 us
    reshape x2, local copies, waits for them, and re-layouts, on_device(): return (new_u.reshape(displacement.shape), acc.reshape(displacement.shape))  1.3 us

profile of v2, /device:TPU:0, one launch (start us, length us, event | category | flops | bytes accessed | tf_op | source)
XLA Modules:
  0.0 60.4 jit_solution(18084376100936995614)
XLA Ops:
  0.6 0.0 copy-start.7
  0.6 0.7 %copy.17 = s32[1,1,2,256]{3,1,2,0:T(1,128)S(1)} copy(s32[1,1,2,256]{3,2,1,0:T(2,128)} %bitcast.12) | data formatting | bytes 4096
  1.4 0.7 %reshape.48 = s32[4,128]{1,0:T(4,128)S(1)} reshape(s32[2,256]{1,0:T(2,128)} %param.22) | data formatting | bytes 4096 | tf_op jit(solution)/shard_map/reshape | solution.py:410
  2.1 0.7 %reshape.50.node = s32[4,512]{1,0:T(4,128)S(1)} reshape(s32[2048]{0:T(1024)} %param.23) | data formatting | bytes 16384 | tf_op jit(solution)/shard_map/reshape | solution.py:453
  2.8 0.7 %reshape.49.owner = s32[4,512]{1,0:T(4,128)S(1)} reshape(s32[2048]{0:T(1024)} %param.24) | data formatting | bytes 16384 | tf_op jit(solution)/shard_map/reshape | solution.py:452
  3.5 0.0 copy-start.8
  3.5 0.7 %reshape.47 = s32[4,512]{1,0:T(4,128)S(1)} reshape(s32[2,1024]{1,0:T(2,128)} %param.25) | data formatting | bytes 16384 | tf_op jit(solution)/shard_map/reshape | solution.py:401
  4.2 0.0 copy-done.7
  4.3 0.0 copy-done.8
  4.3 0.0 copy-start.9
  4.4 0.8 %copy-done.9 = f32[3,4096]{1,0:T(4,128)S(1)} copy-done((f32[3,4096]{1,0:T(4,128)S(1)}, f32[3,4096]{1,0:T(4,128)}, u32[]{:S(2)}) %copy-start.9) | copy-done | bytes 49176
  5.1 0.0 copy-start.10
  5.2 0.8 %copy-done.10 = s32[27,512]{1,0:T(8,128)S(1)} copy-done((s32[27,512]{1,0:T(8,128)S(1)}, s32[27,512]{1,0:T(8,128)}, u32[]{:S(2)}) %copy-start.10) | copy-done | bytes 55320
  6.0 0.0 copy-start
  6.0 0.0 copy-start.1
  6.0 0.0 copy-start.2
  6.0 0.0 copy-start.3
  6.0 0.0 copy-start.4
  6.0 0.0 copy-start.5
  6.0 0.0 copy-start.6
  6.1 0.7 %copy-done = f32[81,81]{1,0:T(8,128)S(1)} copy-done((f32[81,81]{1,0:T(8,128)S(1)}, f32[81,81]{1,0:T(8,128)}, u32[]{:S(2)}) %copy-start) | copy-done | bytes 26268
  6.8 0.0 copy-done.1
  6.8 0.0 copy-done.2
  6.8 0.0 copy-done.3
  6.8 0.0 copy-done.4
  6.8 0.0 copy-done.5
  6.8 0.0 copy-done.6
  6.8 52.3 %contact_steps.1 = (f32[96,128]{1,0:T(8,128)S(1)}, f32[96,128]{1,0:T(8,128)S(1)}) custom-call(s32[40,512]{1,0:T(8,128)S(1)} %select_add_fusion.given_idx, s32[8,128]{1,0:T(8,128)S(1)} %pad.14.lend_idx, s32[4,512]{1,0:T(4,128)S(1)} %reshape.49.owner, s32[4,512]{1,0:T(4,128)S(1)} %reshape.50.node, f32[1,512]{1,0:T(1,128)S(1)} %bitcast.10, ...), custom_call_target="tpu_custom_call" | custom-call | tf_op jit(solution)/shard_map/contact_steps/pallas_call | solution.py:417
  59.1 0.7 %reshape.58 = f32[3,4096]{1,0:T(4,128)} reshape(f32[96,128]{1,0:T(8,128)S(1)} %get-tuple-element.4) | data formatting | bytes 98304 | tf_op jit(solution)/shard_map/reshape | solution.py:465
  59.7 0.7 %reshape.59 = f32[3,4096]{1,0:T(4,128)} reshape(f32[96,128]{1,0:T(8,128)S(1)} %get-tuple-element.5) | data formatting | bytes 98304 | tf_op jit(solution)/shard_map/reshape | solution.py:465
  (5 shorter events, 0.1 us)
Async XLA Ops:
  0.6 3.6 %copy-start.7 = (f32[3,4096]{1,0:T(4,128)S(1)}, f32[3,4096]{1,0:T(4,128)}, u32[]{:S(2)}) copy-start(f32[3,4096]{1,0:T(4,128)} %param.15) | copy-start | bytes 147460
  3.5 0.8 %copy-start.8 = (f32[3,4096]{1,0:T(4,128)S(1)}, f32[3,4096]{1,0:T(4,128)}, u32[]{:S(2)}) copy-start(f32[3,4096]{1,0:T(4,128)} %param.16) | copy-start | bytes 147460
  4.3 0.8 %copy-start.9 = (f32[3,4096]{1,0:T(4,128)S(1)}, f32[3,4096]{1,0:T(4,128)}, u32[]{:S(2)}) copy-start(f32[3,4096]{1,0:T(4,128)} %param.17) | copy-start | bytes 147460
  5.1 0.8 %copy-start.10 = (s32[27,512]{1,0:T(8,128)S(1)}, s32[27,512]{1,0:T(8,128)}, u32[]{:S(2)}) copy-start(s32[27,512]{1,0:T(8,128)} %param.21) | copy-start | bytes 165892
  6.0 0.8 %copy-start = (f32[81,81]{1,0:T(8,128)S(1)}, f32[81,81]{1,0:T(8,128)}, u32[]{:S(2)}) copy-start(f32[81,81]{1,0:T(8,128)} %stiff.1) | copy-start | bytes 78736
  6.0 0.8 %copy-start.1 = (f32[3,1024]{1,0:T(4,128)S(1)}, f32[3,1024]{1,0:T(4,128)}, u32[]{:S(2)}) copy-start(f32[3,1024]{1,0:T(4,128)} %gap0.1) | copy-start | bytes 36868
  6.0 0.8 %copy-start.2 = (s32[3,1024]{1,0:T(4,128)S(1)}, s32[3,1024]{1,0:T(4,128)}, u32[]{:S(2)}) copy-start(s32[3,1024]{1,0:T(4,128)} %slip.1) | copy-start | bytes 36868
  6.0 0.8 %copy-start.3 = (f32[4096]{0:T(1024)S(1)}, f32[4096]{0:T(1024)}, u32[]{:S(2)}) copy-start(f32[4096]{0:T(1024)} %param.18) | copy-start | bytes 49156
  6.0 0.8 %copy-start.4 = (f32[1024]{0:T(1024)S(1)}, f32[1024]{0:T(1024)}, u32[]{:S(2)}) copy-start(f32[1024]{0:T(1024)} %param.27) | copy-start | bytes 12292
  6.0 0.8 %copy-start.5 = (f32[1024]{0:T(1024)S(1)}, f32[1024]{0:T(1024)}, u32[]{:S(2)}) copy-start(f32[1024]{0:T(1024)} %param.28) | copy-start | bytes 12292
  6.0 0.8 %copy-start.6 = (f32[512]{0:T(512)S(1)}, f32[512]{0:T(512)}, u32[]{:S(2)}) copy-start(f32[512]{0:T(512)} %param.19) | copy-start | bytes 6148

commit v3 on v2

--- a/solution.py
+++ b/solution.py
@@ -81,6 +81,7 @@
     recv_tab,
     cur,
     old,
+    load_tab,
     box_out,
     box_in,
     halo_out,
@@ -166,8 +167,12 @@
     for q in range(slots):
         set_row(given + q, numbers[q : q + 1, :])
 
-    cur[...] = disp[...]
-    old[...] = prev[...]
+    for c in range(3):
+        for r in range(own_rows):
+            at, lanes = c * own_rows + r, slice(r * LANES, (r + 1) * LANES)
+            cur[at : at + 1, :] = disp[c : c + 1, lanes]
+            old[at : at + 1, :] = prev[c : c + 1, lanes]
+            load_tab[at : at + 1, :] = load[c : c + 1, lanes]
     ext[...] = jnp.zeros_like(ext)
 
     def box_copy(i, d):
@@ -360,14 +365,16 @@
         for c in range(3):
             rows = slice(c * own_rows, (c + 1) * own_rows)
             internal = ext[c * ext_rows : c * ext_rows + own_rows, :]
-            acceleration = (load[rows, :] - internal + total[rows]) / mass[...]
+            acceleration = (load_tab[rows, :] - internal + total[rows]) / mass[...]
             now = cur[rows, :]
             later = 2.0 * now - old[rows, :] + time_step_sq * acceleration
             old[rows, :] = now
             cur[rows, :] = later
             if step == STEPS - 1:
-                out_u[rows, :] = later
-                out_a[rows, :] = acceleration
+                for r in range(own_rows):
+                    lanes = slice(r * LANES, (r + 1) * LANES)
+                    out_u[c : c + 1, lanes] = later[r : r + 1]
+                    out_a[c : c + 1, lanes] = acceleration[r : r + 1]
 
 
 def on_device(
@@ -416,7 +423,7 @@
     dma = pltpu.SemaphoreType.DMA
     new_u, acc = pl.pallas_call(
         functools.partial(kernel, (n_py, n, cap, elnode, lent, width)),
-        out_shape=[jax.ShapeDtypeStruct(flat, f32)] * 2,
+        out_shape=[jax.ShapeDtypeStruct(displacement.shape, f32)] * 2,
         in_specs=[vmem] * 14,
         out_specs=[vmem] * 2,
         scratch_shapes=[
@@ -431,6 +438,7 @@
             pltpu.VMEM((3, SUBLANES, width), f32),
             pltpu.VMEM((3 * slot_rows, LANES), f32),
             pltpu.VMEM((3 * slot_rows, LANES), f32),
+            pltpu.VMEM(flat, f32),
             pltpu.VMEM(flat, f32),
             pltpu.VMEM(flat, f32),
             pltpu.VMEM((2 * STEPS, n, 3, cap), f32),
@@ -457,12 +465,12 @@
         penalty.reshape(1, -1),
         friction.reshape(1, -1),
         slip_state,
-        displacement.reshape(flat),
-        disp_prev.reshape(flat),
-        nodal_load.reshape(flat),
+        displacement,
+        disp_prev,
+        nodal_load,
         nodal_mass.reshape(-1, LANES),
     )
-    return new_u.reshape(displacement.shape), acc.reshape(displacement.shape)
+    return new_u, acc
 
 
 def solution(mesh):

time: 60.8 us -> 61.9 us (1.018)
  other arithmetic: 0.01 us -> 0.89 us
    unnamed x23 -> x25, local copies, waits for them, and re-layouts: 3.11 us -> 5.51 us
    reshape x5 -> x0, local copies, waits for them, and re-layouts: 1.42 us -> none  [the longest x2 1.3 us: on_device(): return (new_u.reshape(displacement.shape), acc.reshape(displacement.shape))]
    concatenate x1, other arithmetic: 0.01 us -> 0.89 us  [on_device(): jnp.concatenate([jnp.pad(connectivity, ((0, wide - elnode), (0, 0)), cons...]
    reshape x1, local copies, waits for them, and re-layouts: 0.69 us -> 0.01 us  [on_device(): lend_idx = ghost_send.reshape(-1, LANES)]
where the time goes in v3:
time: 61.9 us; the launch traced here: 61.4 us
  Pallas kernels  52.1 us (84%)
  local copies, waits for them, and re-layouts  7.68 us (12%)
  other arithmetic  0.89 us (1%)
  between operations  0.74 us (1%)
    pallas_call x1, Pallas kernels, on_device(): pl.pallas_call(functools.partial(kernel, (n_py, n, cap, elnode, lent, wid...  52.1 us
    unnamed x25, local copies, waits for them, and re-layouts  5.51 us

profile of v3, /device:TPU:0, one launch (start us, length us, event | category | flops | bytes accessed | tf_op | source)
XLA Modules:
  0.0 61.4 jit_solution(4463773227451176042)
XLA Ops:
  0.6 0.0 copy-start.10
  0.6 0.0 copy-start.5
  0.6 0.7 %copy-done.10 = s32[2,256]{1,0:T(2,128)S(1)} copy-done((s32[2,256]{1,0:T(2,128)S(1)}, s32[2,256]{1,0:T(2,128)}, u32[]{:S(2)}) %copy-start.10) | copy-done | bytes 2072
  1.3 0.0 copy-start.4
  1.3 0.0 copy-start.2
  1.4 0.7 %reshape.35.node = s32[4,512]{1,0:T(4,128)S(1)} reshape(s32[2048]{0:T(1024)} %param.23) | data formatting | bytes 16384 | tf_op jit(solution)/shard_map/reshape | solution.py:461
  2.1 0.7 %reshape.34.owner = s32[4,512]{1,0:T(4,128)S(1)} reshape(s32[2048]{0:T(1024)} %param.24) | data formatting | bytes 16384 | tf_op jit(solution)/shard_map/reshape | solution.py:460
  2.8 0.7 %reshape.32 = s32[4,512]{1,0:T(4,128)S(1)} reshape(s32[2,1024]{1,0:T(2,128)} %param.25) | data formatting | bytes 16384 | tf_op jit(solution)/shard_map/reshape | solution.py:408
  3.5 0.0 copy-start
  3.5 0.0 copy-start.1
  3.5 0.9 %select_add_fusion.given_idx = s32[40,512]{1,0:T(8,128)S(1)} fusion(s32[4,512]{1,0:T(4,128)S(1)} %reshape.32, s32[27,512]{1,0:T(8,128)} %param.21, s32[1,512]{1,0:T(1,128)S(1)} %bitcast.11), kind=kLoop, calls=%fused_computation | loop fusion | flops 122880 | bytes 147456 | tf_op jit(solution)/shard_map/concatenate | solution.py:409
  4.4 0.0 copy-done.5
  4.4 0.0 copy-done.4
  4.4 0.0 copy-done.2
  4.4 0.0 copy-done
  4.5 0.0 copy-done.1
  4.5 0.0 copy-start.3
  4.5 0.8 %copy-done.3 = f32[81,81]{1,0:T(8,128)S(1)} copy-done((f32[81,81]{1,0:T(8,128)S(1)}, f32[81,81]{1,0:T(8,128)}, u32[]{:S(2)}) %copy-start.3) | copy-done | bytes 26268
  5.3 0.0 copy-start.6
  5.3 0.7 %copy-done.6 = f32[4096]{0:T(1024)S(1)} copy-done((f32[4096]{0:T(1024)S(1)}, f32[4096]{0:T(1024)}, u32[]{:S(2)}) %copy-start.6) | copy-done | bytes 16408
  6.0 0.0 copy-start.7
  6.0 0.7 %copy-done.7 = f32[1024]{0:T(1024)S(1)} copy-done((f32[1024]{0:T(1024)S(1)}, f32[1024]{0:T(1024)}, u32[]{:S(2)}) %copy-start.7) | copy-done | bytes 4120
  6.7 0.0 copy-start.8
  6.7 0.7 %copy-done.8 = f32[1024]{0:T(1024)S(1)} copy-done((f32[1024]{0:T(1024)S(1)}, f32[1024]{0:T(1024)}, u32[]{:S(2)}) %copy-start.8) | copy-done | bytes 4120
  7.4 0.0 copy-start.9
  7.4 0.7 %copy-done.9 = f32[512]{0:T(512)S(1)} copy-done((f32[512]{0:T(512)S(1)}, f32[512]{0:T(512)}, u32[]{:S(2)}) %copy-start.9) | copy-done | bytes 2072
  8.0 52.1 %contact_steps.1 = (f32[3,4096]{1,0:T(4,128)S(1)}, f32[3,4096]{1,0:T(4,128)S(1)}) custom-call(s32[40,512]{1,0:T(8,128)S(1)} %select_add_fusion.given_idx, s32[8,128]{1,0:T(8,128)S(1)} %pad.14.lend_idx, s32[4,512]{1,0:T(4,128)S(1)} %reshape.34.owner, s32[4,512]{1,0:T(4,128)S(1)} %reshape.35.node, f32[1,512]{1,0:T(1,128)S(1)} %bitcast.10, ...), custom_call_target="tpu_custom_call" | custom-call | tf_op jit(solution)/shard_map/contact_steps/pallas_call | solution.py:424
  60.1 0.6 %copy.20 = f32[3,4096]{1,0:T(4,128)} copy(f32[3,4096]{1,0:T(4,128)S(1)} %get-tuple-element.4) | data formatting | bytes 98304
  60.7 0.6 %copy.21 = f32[3,4096]{1,0:T(4,128)} copy(f32[3,4096]{1,0:T(4,128)S(1)} %get-tuple-element.5) | data formatting | bytes 98304
  (3 shorter events, 0.0 us)
Async XLA Ops:
  0.6 0.7 %copy-start.10 = (s32[2,256]{1,0:T(2,128)S(1)}, s32[2,256]{1,0:T(2,128)}, u32[]{:S(2)}) copy-start(s32[2,256]{1,0:T(2,128)} %param.22) | copy-start | bytes 6148
  0.6 3.8 %copy-start.5 = (s32[3,1024]{1,0:T(4,128)S(1)}, s32[3,1024]{1,0:T(4,128)}, u32[]{:S(2)}) copy-start(s32[3,1024]{1,0:T(4,128)} %slip.1) | copy-start | bytes 36868
  1.3 3.1 %copy-start.4 = (f32[3,1024]{1,0:T(4,128)S(1)}, f32[3,1024]{1,0:T(4,128)}, u32[]{:S(2)}) copy-start(f32[3,1024]{1,0:T(4,128)} %gap0.1) | copy-start | bytes 36868
  1.3 3.1 %copy-start.2 = (f32[3,4096]{1,0:T(4,128)S(1)}, f32[3,4096]{1,0:T(4,128)}, u32[]{:S(2)}) copy-start(f32[3,4096]{1,0:T(4,128)} %load.1) | copy-start | bytes 147460
  3.5 0.9 %copy-start = (f32[3,4096]{1,0:T(4,128)S(1)}, f32[3,4096]{1,0:T(4,128)}, u32[]{:S(2)}) copy-start(f32[3,4096]{1,0:T(4,128)} %disp.1) | copy-start | bytes 147460
  3.5 0.9 %copy-start.1 = (f32[3,4096]{1,0:T(4,128)S(1)}, f32[3,4096]{1,0:T(4,128)}, u32[]{:S(2)}) copy-start(f32[3,4096]{1,0:T(4,128)} %prev.1) | copy-start | bytes 147460
  4.5 0.8 %copy-start.3 = (f32[81,81]{1,0:T(8,128)S(1)}, f32[81,81]{1,0:T(8,128)}, u32[]{:S(2)}) copy-start(f32[81,81]{1,0:T(8,128)} %stiff.1) | copy-start | bytes 78736
  5.3 0.7 %copy-start.6 = (f32[4096]{0:T(1024)S(1)}, f32[4096]{0:T(1024)}, u32[]{:S(2)}) copy-start(f32[4096]{0:T(1024)} %param.18) | copy-start | bytes 49156
  6.0 0.7 %copy-start.7 = (f32[1024]{0:T(1024)S(1)}, f32[1024]{0:T(1024)}, u32[]{:S(2)}) copy-start(f32[1024]{0:T(1024)} %param.27) | copy-start | bytes 12292
  6.7 0.7 %copy-start.8 = (f32[1024]{0:T(1024)S(1)}, f32[1024]{0:T(1024)}, u32[]{:S(2)}) copy-start(f32[1024]{0:T(1024)} %param.28) | copy-start | bytes 12292
  7.4 0.7 %copy-start.9 = (f32[512]{0:T(512)S(1)}, f32[512]{0:T(512)}, u32[]{:S(2)}) copy-start(f32[512]{0:T(512)} %param.19) | copy-start | bytes 6148
